TPU v7x, 32 devices: a whole 2x2x4 slice. The times are simulated.
32 devices in a mesh: grp: 8 (over y, x, core), top: 4 (over z).
Axes of the slice: x: 2, y: 2, z: 4, core: 2. Of those that a mesh axis runs over, the one named last changes fastest.
Arguments:
- basis_grad: float32 [8, 4, 512, 384], P('grp', 'top'), may hold values from -6 to 6
- leaf_q: float32 [8, 4, 512, 384], P('grp', 'top'), may hold values from -0.25 to 0.25
- leaf_rinv: float32 [8, 4, 384, 384], P('grp', 'top'), may hold values from -5 to 4, as said below
- merge_q1: float32 [8, 4, 384, 384], P('grp', 'top'), may hold values from -0.3125 to 0.3125
- merge_q2: float32 [4, 384, 384], P('top', 'grp'), may hold values from -0.15625 to 0.15625
Outputs:
- data_grad: float32 [8, 4, 512, 384], P('grp', 'top')
Inputs may be any that keep to these rules, and one draw needn't show every extreme that they name: Each leaf_rinv[i,g] is upper triangular with a diagonal between 1 and 4.
All inputs are finite; a program needn't handle non-finite values.
Results may differ from a plain program's by a relative error of at most 0.00023.
Values sent between devices are 32-bit elements; how exact they have to be, the bound alone decides.
A program may use at most 64 MiB of HBM per device.

v0:
```python
import jax
import jax.numpy as jnp
from jax import lax
from jax.sharding import PartitionSpec as P


def product(former, latter, former_dim, latter_dim):
    return lax.dot_general(
        former,
        latter,
        (((former_dim,), (latter_dim,)), ((), ())),
        precision=lax.Precision.HIGH,
        preferred_element_type=jnp.float32,
    )


def symmetrize(matrix):
    return jnp.tril(matrix) + jnp.tril(matrix, -1).T


def per_device(basis_grad, leaf_q, leaf_rinv, merge_q1, merge_q2):
    cotangent = basis_grad[0, 0]
    leaf_basis = leaf_q[0, 0]
    inverse = leaf_rinv[0, 0]
    first_block = merge_q1[0, 0]
    second_factor = lax.all_gather(merge_q2[0], "grp", axis=0, tiled=True)
    projected = product(leaf_basis, cotangent, 0, 0)
    combined = product(first_block, second_factor, 1, 0)
    top_adjoint = -lax.psum(product(projected, combined, 0, 0), ("grp", "top"))
    top_sym = symmetrize(top_adjoint)
    spread = product(leaf_basis, combined, 1, 0)
    outer = product(inverse, combined, 1, 0)
    inner = cotangent + product(spread, top_sym, 1, 0)
    result = product(inner, outer, 1, 1)
    return result[None, None]


def solution(mesh):
    placed = (
        P("grp", "top", None, None),
        P("grp", "top", None, None),
        P("grp", "top", None, None),
        P("grp", "top", None, None),
        P("top", "grp", None),
    )
    return jax.shard_map(
        per_device,
        mesh=mesh,
        in_specs=placed,
        out_specs=P("grp", "top", None, None),
        check_vma=False,
    )
```

profile of v0, /device:TPU:0, one launch (start us, length us, event | category | flops | bytes accessed | tf_op | source)
XLA Modules:
  0.0 163.3 jit_solution(13517483141683757118)
XLA Ops:
  6.5 0.0 copy-start
  6.5 0.0 copy-start.2
  6.5 0.0 all-reduce.2.cloned.1.call-start
  6.5 11.9 %all-gather = f32[1,384,384]{2,1,0:T(8,128)S(1)} all-gather(f32[1,48,384]{2,1,0:T(8,128)} %param.9), channel_id=2, replica_groups=mesh['grp'=8,'top'=4] {'grp'}, dimensions={1}, use_global_device_ids=true | all-gather | bytes 663552 | tf_op jit(solution)/shard_map/all_gather | solution.py:26
  18.4 0.0 copy-done.2
  18.4 0.0 copy-start.1
  18.4 0.7 fusion.7
  19.2 0.0 copy-done
  19.2 0.4 copy-done.1
  19.6 0.8 fusion
  20.4 1.6 fusion.17
  22.0 0.0 copy-start.3
  22.0 0.0 all-reduce.2.cloned.1.call-update
  22.0 1.0 copy-done.3
  23.0 1.1 fusion.5
  24.2 1.2 fusion.2
  25.3 124.4 %all-reduce.2.cloned.1.call-done = f32[384,384]{1,0:T(8,128)} async-done(((f32[384,384]{1,0:T(8,128)}), f32[384,384]{1,0:T(8,128)}) %all-reduce.2.cloned.1.call-update) | async-done | bytes 589840 | tf_op jit(solution)/shard_map/psum | solution.py:29
  149.8 1.1 neg.3
  150.9 1.1 copy.6
  151.9 2.7 %convolution_add_fusion = f32[512,384]{1,0:T(8,128)S(1)} fusion(f32[384,512]{1,0:T(8,128)S(1)} %fusion.2, f32[1,1,512,384]{3,2,1,0:T(8,128)S(1)} %copy-done.1, f32[384,384]{0,1:T(8,128)} %copy.6, s32[384]{0:T(512)S(1)} %iota_add_fusion, f32[384,384]{1,0:T(8,128)} %all-reduce.2.cloned.1.call-done), kind=kOutput, calls=%fused_computation.1 | convolution fusion | flops 454066176 | bytes 3540480 | tf_op jit(solution)/shard_map/dot_general | solution.py:8
  154.7 1.8 %convolution_bitcast_fusion = f32[1,1,512,384]{3,2,1,0:T(8,128)} fusion(f32[512,384]{1,0:T(8,128)S(1)} %convolution_add_fusion, f32[384,384]{1,0:T(8,128)S(1)} %fusion.5), kind=kOutput, calls=%fused_computation | convolution fusion | flops 452984832 | bytes 2162688 | tf_op jit(solution)/shard_map/dot_general | solution.py:8
  (1 shorter events, 0.0 us)
Async XLA Ops:
  6.5 12.6 %copy-start = (f32[1,1,512,384]{3,2,1,0:T(8,128)S(1)}, f32[1,1,512,384]{3,2,1,0:T(8,128)}, u32[]{:S(2)}) copy-start(f32[1,1,512,384]{3,2,1,0:T(8,128)} %param.6) | copy-start | bytes 2359300
  6.5 11.9 %copy-start.2 = (f32[1,1,384,384]{3,2,1,0:T(8,128)S(1)}, f32[1,1,384,384]{3,2,1,0:T(8,128)}, u32[]{:S(2)}) copy-start(f32[1,1,384,384]{3,2,1,0:T(8,128)} %param.8) | copy-start | bytes 1769476
  6.5 143.2 %all-reduce.2.cloned.1.call-start = ((), (), s32[]{:S(2)}) async-start(), calls=%async_computation | async-start | bytes 1179648 | tf_op jit(solution)/shard_map/psum | solution.py:29
  18.4 1.1 copy-start.1
  22.0 1.1 copy-start.3
Sparse Core Ops, SparseCore 0:
  22.1 127.6 all-reduce.1
where the time goes:
time: 164 us; the launch traced here: 163 us
  waiting for transfers between devices  124 us (76%)
  between operations  13.4 us (8%)
  blocking collectives  11.9 us (7%)
  matrix products  9.86 us (6%)
  local copies, waits for them, and re-layouts  2.51 us (2%)
    psum x1, waiting for transfers between devices, per_device(): top_adjoint = -lax.psum(product(projected, combined, 0, 0), ('grp', 'top'))  124 us
    all_gather x1, blocking collectives, per_device(): second_factor = lax.all_gather(merge_q2[0], 'grp', axis=0, tiled=True)  11.9 us
    dot_general x7, matrix products, product(): lax.dot_general(former, latter, (((former_dim,), (latter_dim,)), ((), ())...  9.86 us
  transfers between devices with their start and end apart: 1, of which 1 were waited for; matrix products, arithmetic and copies ran while one was open for 1% of the time, Pallas kernels for 0%

commit v1 on v0

--- a/solution.py
+++ b/solution.py
@@ -1,7 +1,15 @@
+import functools
 import jax
 import jax.numpy as jnp
 from jax import lax
 from jax.sharding import PartitionSpec as P
+
+
+def mix_keys_for(x0, axis_name):
+    return lax.all_gather(x0, axis_name=axis_name).sum(axis=0)
+
+
+map_cycles_now = functools.partial(mix_keys_for, axis_name=("grp", "top"))
 
 
 def product(former, latter, former_dim, latter_dim):
@@ -26,7 +34,7 @@
     second_factor = lax.all_gather(merge_q2[0], "grp", axis=0, tiled=True)
     projected = product(leaf_basis, cotangent, 0, 0)
     combined = product(first_block, second_factor, 1, 0)
-    top_adjoint = -lax.psum(product(projected, combined, 0, 0), ("grp", "top"))
+    top_adjoint = -map_cycles_now(product(projected, combined, 0, 0))
     top_sym = symmetrize(top_adjoint)
     spread = product(leaf_basis, combined, 1, 0)
     outer = product(inverse, combined, 1, 0)

time: 164 us -> 171 us (1.043)
  other arithmetic: 1.11 us -> 8.12 us
  matrix products: 9.86 us -> 13 us
  waiting for transfers between devices: 124 us -> 122 us
    psum x1 -> x0, waiting for transfers between devices: 124 us -> none  [per_device(): top_adjoint = -lax.psum(product(projected, combined, 0, 0), ('grp', 'top'))]
    all_gather x0 -> x1, waiting for transfers between devices: none -> 122 us  [mix_keys_for(): return lax.all_gather(x0, axis_name=axis_name).sum(axis=0)]
    reduce_sum x0 -> x1, other arithmetic: none -> 7.26 us  [mix_keys_for(): return lax.all_gather(x0, axis_name=axis_name).sum(axis=0)]
    dot_general x7, matrix products: 9.86 us -> 13 us  [product(): lax.dot_general(former, latter, (((former_dim,), (latter_dim,)), ((), ())...]
  transfers between devices with their start and end apart: 1 -> 1, of which waited for: 1 -> 1; matrix products, arithmetic and copies ran while one was open for 1% -> 2% of each run, Pallas kernels for 0% -> 0%
where the time goes in v1:
time: 171 us; the launch traced here: 170 us
  waiting for transfers between devices  122 us (71%)
  between operations  13.4 us (8%)
  matrix products  13 us (8%)
  blocking collectives  11.9 us (7%)
  other arithmetic  8.12 us (5%)
  local copies, waits for them, and re-layouts  2.12 us (1%)
    all_gather x1, waiting for transfers between devices, mix_keys_for(): return lax.all_gather(x0, axis_name=axis_name).sum(axis=0)  122 us
    dot_general x7, matrix products, product(): lax.dot_general(former, latter, (((former_dim,), (latter_dim,)), ((), ())...  13 us
    all_gather x1, blocking collectives, per_device(): second_factor = lax.all_gather(merge_q2[0], 'grp', axis=0, tiled=True)  11.9 us
    reduce_sum x1, other arithmetic, mix_keys_for(): return lax.all_gather(x0, axis_name=axis_name).sum(axis=0)  7.26 us
  transfers between devices with their start and end apart: 1, of which 1 were waited for; matrix products, arithmetic and copies ran while one was open for 2% of the time, Pallas kernels for 0%

profile of v1, /device:TPU:0, one launch (start us, length us, event | category | flops | bytes accessed | tf_op | source)
XLA Modules:
  0.0 170.3 jit_solution(14252127622664350674)
XLA Ops:
  6.5 0.0 copy-start
  6.5 0.0 copy-start.1
  6.5 0.0 all-gather.4.cloned.1.call-start
  6.5 11.9 %all-gather = f32[1,384,384]{2,1,0:T(8,128)S(1)} all-gather(f32[1,48,384]{2,1,0:T(8,128)} %param.9), channel_id=2, replica_groups=mesh['grp'=8,'top'=4] {'grp'}, dimensions={1}, use_global_device_ids=true | all-gather | bytes 663552 | tf_op jit(solution)/shard_map/all_gather | solution.py:34
  18.4 1.8 %fusion.9 = f32[384,384]{1,0:T(8,128)S(1)} fusion(f32[1,384,384]{2,1,0:T(8,128)S(1)} %all-gather, f32[1,1,384,384]{3,2,1,0:T(8,128)} %param.8), kind=kOutput, calls=%fused_computation.11 | convolution fusion | flops 339738624 | bytes 1769472 | tf_op jit(solution)/shard_map/dot_general | solution.py:16
  20.2 0.0 copy-done
  20.2 1.9 %fusion = f32[384,384]{1,0:T(8,128)S(1)} fusion(f32[1,1,512,384]{3,2,1,0:T(8,128)S(1)} %copy-done, f32[1,1,512,384]{3,2,1,0:T(8,128)} %param.5), kind=kOutput, calls=%fused_computation.2 | convolution fusion | flops 452984832 | bytes 2162688 | tf_op jit(solution)/shard_map/dot_general | solution.py:16
  22.2 1.6 fusion.17
  23.8 0.0 all-gather.4.cloned.1.call-update
  23.8 2.2 %fusion.5 = f32[384,384]{1,0:T(8,128)S(1)} fusion(f32[384,384]{1,0:T(8,128)S(1)} %fusion.9, f32[1,1,384,384]{3,2,1,0:T(8,128)} %param.7), kind=kOutput, calls=%fused_computation.7 | convolution fusion | flops 339738624 | bytes 1769472 | tf_op jit(solution)/shard_map/dot_general | solution.py:16
  26.0 1.2 fusion.2
  27.1 121.8 %all-gather.4.cloned.1.call-done = f32[12288,384]{1,0:T(8,128)} async-done(((f32[384,384]{1,0:T(8,128)}), f32[12288,384]{1,0:T(8,128)}) %all-gather.4.cloned.1.call-update) | async-done | bytes 18874384 | tf_op jit(solution)/shard_map/all_gather | solution.py:9
  148.9 7.3 %reduce_sum.9 = f32[384,384]{1,0:T(8,128)S(1)} reduce(f32[32,384,384]{2,1,0:T(8,128)} %bitcast.33, f32[]{:T(128)} %constant.4.clone.1), dimensions={0}, to_apply=%region_0.0 | reduce | flops 4571136 | bytes 19464196 | tf_op jit(solution)/shard_map/reduce_sum | solution.py:9
  156.2 0.9 neg.7
  157.0 2.1 %copy.7 = f32[384,384]{0,1:T(8,128)} copy(f32[384,384]{1,0:T(8,128)} %neg.7) | data formatting | bytes 1179648 | tf_op jit(solution)/shard_map/neg | solution.py:37
  159.1 0.0 copy-done.1
  159.1 2.6 %convolution_add_fusion = f32[512,384]{1,0:T(8,128)S(1)} fusion(f32[384,512]{1,0:T(8,128)S(1)} %fusion.2, f32[1,1,512,384]{3,2,1,0:T(8,128)S(1)} %copy-done.1, f32[384,384]{0,1:T(8,128)} %copy.7, s32[384]{0:T(512)S(1)} %iota_add_fusion, f32[384,384]{1,0:T(8,128)S(1)} %reduce_sum.9), kind=kOutput, calls=%fused_computation.1 | convolution fusion | flops 454066176 | bytes 3540480 | tf_op jit(solution)/shard_map/dot_general | solution.py:16
  161.7 1.8 %convolution_bitcast_fusion = f32[1,1,512,384]{3,2,1,0:T(8,128)} fusion(f32[512,384]{1,0:T(8,128)S(1)} %convolution_add_fusion, f32[384,384]{1,0:T(8,128)S(1)} %fusion.5), kind=kOutput, calls=%fused_computation | convolution fusion | flops 452984832 | bytes 2162688 | tf_op jit(solution)/shard_map/dot_general | solution.py:16
  (1 shorter events, 0.0 us)
Async XLA Ops:
  6.5 13.7 %copy-start = (f32[1,1,512,384]{3,2,1,0:T(8,128)S(1)}, f32[1,1,512,384]{3,2,1,0:T(8,128)}, u32[]{:S(2)}) copy-start(f32[1,1,512,384]{3,2,1,0:T(8,128)} %param.6) | copy-start | bytes 2359300
  6.5 152.6 %copy-start.1 = (f32[1,1,512,384]{3,2,1,0:T(8,128)S(1)}, f32[1,1,512,384]{3,2,1,0:T(8,128)}, u32[]{:S(2)}) copy-start(f32[1,1,512,384]{3,2,1,0:T(8,128)} %param.5) | copy-start | bytes 2359300
  6.5 142.4 %all-gather.4.cloned.1.call-start = ((), (), s32[]{:S(2)}) async-start(), calls=%async_computation | async-start | bytes 19464192 | tf_op jit(solution)/shard_map/all_gather | solution.py:9
Sparse Core Ops, SparseCore 0:
  23.9 124.9 all-gather.3
